TPU v7x, 32 devices: a whole 2x2x4 slice. The times are simulated.
32 devices in a mesh: fsdp: 2 (over core), ctx: 4 (over y, x), tp: 4 (over z).
Axes of the slice: x: 2, y: 2, z: 4, core: 2. Of those that a mesh axis runs over, the one named last changes fastest.
Arguments:
- x_prompt: bfloat16 [2, 1024, 1024], P('fsdp', 'ctx'), may hold values from -6 to 6
- x_cont: bfloat16 [2, 12, 256, 1024], P('fsdp', 'ctx'), may hold values from -6 to 6
- cont_start: int32 [2, 12], P('fsdp', 'ctx'), may hold values from 512 to 1024
- w_qkv: bfloat16 [1024, 3, 1024], P(('fsdp', 'ctx'), None, 'tp'), may hold values from -0.1875 to 0.1875
- qkv_bias: bfloat16 [3, 1024], P(None, 'tp'), may hold values from -3 to 3
- w_dense: bfloat16 [1024, 1024], P('tp', ('fsdp', 'ctx')), may hold values from -0.75 to 0.75
- dense_bias: bfloat16 [1024], P(('fsdp', 'ctx')), may hold values from -3 to 3
- w_fc1: bfloat16 [1024, 4096], P(('fsdp', 'ctx'), 'tp'), may hold values from -0.1875 to 0.1875
- fc1_bias: bfloat16 [4096], P('tp'), may hold values from -3 to 3
- w_fc2: bfloat16 [4096, 1024], P('tp', ('fsdp', 'ctx')), may hold values from -0.09375 to 0.09375
- fc2_bias: bfloat16 [1024], P(('fsdp', 'ctx')), may hold values from -3 to 3
- ln1_gain: bfloat16 [1024], P(('fsdp', 'ctx')), may hold values from 0.099609375 to 1.8984375
- ln1_bias: bfloat16 [1024], P(('fsdp', 'ctx')), may hold values from -2 to 2
- ln2_gain: bfloat16 [1024], P(('fsdp', 'ctx')), may hold values from 0.099609375 to 1.8984375
- ln2_bias: bfloat16 [1024], P(('fsdp', 'ctx')), may hold values from -2 to 2
- dy_prompt: bfloat16 [2, 1024, 1024], P('fsdp', 'ctx'), may hold values from -6 to 6
- dy_cont: bfloat16 [2, 12, 256, 1024], P('fsdp', 'ctx'), may hold values from -6 to 6
Outputs:
- y_prompt: float32 [2, 1024, 1024], P('fsdp', 'ctx')
- y_cont: float32 [2, 12, 256, 1024], P('fsdp', 'ctx')
- dx_prompt: float32 [2, 1024, 1024], P('fsdp', 'ctx')
- dx_cont: float32 [2, 12, 256, 1024], P('fsdp', 'ctx')
- d_w_qkv: float32 [1024, 3, 1024], P(('fsdp', 'ctx'), None, 'tp')
- d_qkv_bias: float32 [3, 1024], P(None, 'tp')
- d_w_dense: float32 [1024, 1024], P('tp', ('fsdp', 'ctx'))
- d_dense_bias: float32 [1024], P(('fsdp', 'ctx'))
- d_w_fc1: float32 [1024, 4096], P(('fsdp', 'ctx'), 'tp')
- d_fc1_bias: float32 [4096], P('tp')
- d_w_fc2: float32 [4096, 1024], P('tp', ('fsdp', 'ctx'))
- d_fc2_bias: float32 [1024], P(('fsdp', 'ctx'))
- d_ln1_gain: float32 [1024], P(('fsdp', 'ctx'))
- d_ln1_bias: float32 [1024], P(('fsdp', 'ctx'))
- d_ln2_gain: float32 [1024], P(('fsdp', 'ctx'))
- d_ln2_bias: float32 [1024], P(('fsdp', 'ctx'))
Inputs may be any that keep to these rules, and one draw needn't show every extreme that they name: `cont_start`: a continuation follows the prompt tokens before its first position.
All inputs are finite; a program needn't handle non-finite values.
Results may differ from a plain program's by a relative error of at most 0.012.
Values may be sent and summed in bfloat16 or wider, within the bound.
A program may use at most 192 MiB of HBM per device.

v0:
```python
import jax
import jax.numpy as jnp
from jax import lax
from jax.sharding import PartitionSpec as P

HD = 64
ROT = 16
EPS = 1e-05


def layer_norm(inputs, norm_gain, norm_shift):
    row_mean = jnp.mean(inputs, axis=-1, keepdims=True)
    centered = inputs - row_mean
    variance = jnp.mean(centered * centered, axis=-1, keepdims=True)
    return centered * lax.rsqrt(variance + EPS) * norm_gain + norm_shift


def norm_pair(inputs, gain_one, shift_one, gain_two, shift_two):
    return (layer_norm(inputs, gain_one, shift_one), layer_norm(inputs, gain_two, shift_two))


def exact_gelu(values):
    return jax.nn.gelu(values, approximate=False)


def rotary_tables(positions):
    freq_index = jnp.arange(ROT // 2).astype(jnp.float32)
    inverse = jnp.power(10000.0, -2.0 * freq_index / ROT)
    phase = positions.astype(jnp.float32)[..., None] * inverse
    cos_half = jnp.cos(phase)
    sin_half = jnp.sin(phase)
    return (
        jnp.concatenate([cos_half, cos_half], axis=-1),
        jnp.concatenate([sin_half, sin_half], axis=-1),
    )


def rotate(inputs, cos_t, sin_t):
    leading = inputs[..., :ROT]
    half_rot = ROT // 2
    turned = jnp.concatenate([-leading[..., half_rot:], leading[..., :half_rot]], axis=-1)
    return jnp.concatenate([leading * cos_t + turned * sin_t, inputs[..., ROT:]], axis=-1)


def masked_scores(
    queries, all_keys, key_limit, query_slot, query_offs, prompt_len, key_slot, key_offs
):
    raw_scores = jnp.einsum("qhd,khd->hqk", queries, all_keys, preferred_element_type=jnp.float32)
    key_index = jnp.arange(all_keys.shape[0], dtype=jnp.int32)
    near_keys = key_index[None, :] < key_limit[:, None]
    own_keys = (key_slot[None, :] == query_slot[:, None]) & (
        key_offs[None, :] <= query_offs[:, None]
    )
    allowed = jnp.where((key_index < prompt_len)[None, :], near_keys, own_keys)
    return jnp.where(allowed[None], raw_scores * 0.125, -1e30)


def on_device(
    x_prompt,
    x_cont,
    cont_start,
    w_qkv,
    qkv_bias,
    w_dense,
    dense_bias,
    w_fc1,
    fc1_bias,
    w_fc2,
    fc2_bias,
    ln1_gain,
    ln1_bias,
    ln2_gain,
    ln2_bias,
    dy_prompt,
    dy_cont,
):
    gathered = (
        lax.all_gather(w_qkv, ("fsdp", "ctx"), axis=0, tiled=True),
        lax.all_gather(w_dense, ("fsdp", "ctx"), axis=1, tiled=True),
        lax.all_gather(w_fc1, ("fsdp", "ctx"), axis=0, tiled=True),
        lax.all_gather(w_fc2, ("fsdp", "ctx"), axis=1, tiled=True),
        lax.all_gather(dense_bias, ("fsdp", "ctx"), axis=0, tiled=True),
        lax.all_gather(fc2_bias, ("fsdp", "ctx"), axis=0, tiled=True),
        lax.all_gather(ln1_gain, ("fsdp", "ctx"), axis=0, tiled=True),
        lax.all_gather(ln1_bias, ("fsdp", "ctx"), axis=0, tiled=True),
        lax.all_gather(ln2_gain, ("fsdp", "ctx"), axis=0, tiled=True),
        lax.all_gather(ln2_bias, ("fsdp", "ctx"), axis=0, tiled=True),
    )
    qkv_full, dense_full, up_full, down_full = (gathered[0], gathered[1], gathered[2], gathered[3])
    dense_shift = gathered[4].astype(jnp.float32)
    down_shift = gathered[5].astype(jnp.float32)
    gain_one = gathered[6].astype(jnp.float32)
    shift_one = gathered[7].astype(jnp.float32)
    gain_two = gathered[8].astype(jnp.float32)
    shift_two = gathered[9].astype(jnp.float32)
    p_rows = x_prompt.shape[1]
    cont_count = x_cont.shape[1]
    cont_len = x_cont.shape[2]
    model_width = x_prompt.shape[2]
    row_count = p_rows + cont_count * cont_len
    prompt_len = p_rows * lax.axis_size("ctx")
    local_cols = qkv_full.shape[2]
    head_count = local_cols // HD
    piece_index = lax.axis_index("ctx")
    inputs = jnp.concatenate(
        [x_prompt[0], x_cont[0].reshape(cont_count * cont_len, model_width)], axis=0
    ).astype(jnp.float32)
    offsets = jnp.arange(cont_len, dtype=jnp.int32)
    prompt_pos = piece_index * p_rows + jnp.arange(p_rows, dtype=jnp.int32)
    starts = cont_start[0]
    cont_pos = (starts[:, None] + offsets[None, :]).reshape(cont_count * cont_len)
    positions = jnp.concatenate([prompt_pos, cont_pos])
    key_limit = jnp.concatenate([prompt_pos + 1, jnp.repeat(starts, cont_len)])
    own_slot = jnp.repeat(jnp.arange(cont_count, dtype=jnp.int32), cont_len)
    own_offs = jnp.tile(offsets, cont_count)
    query_slot = jnp.concatenate([jnp.full((p_rows,), -1, jnp.int32), own_slot])
    query_offs = jnp.concatenate([jnp.zeros((p_rows,), jnp.int32), own_offs])
    key_slot = jnp.concatenate([jnp.full((prompt_len,), -1, jnp.int32), own_slot])
    key_offs = jnp.concatenate([jnp.zeros((prompt_len,), jnp.int32), own_offs])
    cos_t, sin_t = rotary_tables(positions)
    cos_t = cos_t[:, None, :]
    sin_t = sin_t[:, None, :]
    norm_one, norm_two = norm_pair(inputs, gain_one, shift_one, gain_two, shift_two)
    ln_one = norm_one.astype(jnp.bfloat16)
    ln_two = norm_two.astype(jnp.bfloat16)
    qkv_flat = qkv_full.reshape(model_width, 3 * local_cols)
    projected = jnp.dot(ln_one, qkv_flat, preferred_element_type=jnp.float32) + qkv_bias.reshape(
        3 * local_cols
    ).astype(jnp.float32)
    projected = projected.reshape(row_count, 3, head_count, HD)
    queries = rotate(projected[:, 0], cos_t, sin_t).astype(jnp.bfloat16)
    keys_own = rotate(projected[:, 1], cos_t, sin_t).astype(jnp.bfloat16)
    values_own = projected[:, 2].astype(jnp.bfloat16)
    prompt_keys, prompt_values = (
        lax.all_gather(keys_own[:p_rows].reshape(p_rows, local_cols), "ctx", axis=0, tiled=True),
        lax.all_gather(values_own[:p_rows].reshape(p_rows, local_cols), "ctx", axis=0, tiled=True),
    )
    all_keys = jnp.concatenate(
        [prompt_keys.reshape(prompt_len, head_count, HD), keys_own[p_rows:]], axis=0
    )
    all_values = jnp.concatenate(
        [prompt_values.reshape(prompt_len, head_count, HD), values_own[p_rows:]], axis=0
    )
    scores = masked_scores(
        queries, all_keys, key_limit, query_slot, query_offs, prompt_len, key_slot, key_offs
    )
    highest = jnp.max(scores, axis=-1, keepdims=True)
    log_total = highest + jnp.log(jnp.sum(jnp.exp(scores - highest), axis=-1, keepdims=True))
    probs_low = jnp.exp(scores - log_total).astype(jnp.bfloat16)
    attended = jnp.einsum("hqk,khd->qhd", probs_low, all_values, preferred_element_type=jnp.float32)
    attended_low = attended.reshape(row_count, local_cols).astype(jnp.bfloat16)
    attn_part = jnp.dot(attended_low, dense_full, preferred_element_type=jnp.float32)
    hidden = jnp.dot(ln_two, up_full, preferred_element_type=jnp.float32) + fc1_bias.astype(
        jnp.float32
    )
    active_low = exact_gelu(hidden).astype(jnp.bfloat16)
    mlp_part = jnp.dot(active_low, down_full, preferred_element_type=jnp.float32)
    attn_total = lax.psum(attn_part, "tp")
    mlp_total = lax.psum(mlp_part.astype(jnp.bfloat16), "tp").astype(jnp.float32)
    mixed = attn_total + mlp_total
    output = inputs + mixed + dense_shift + down_shift
    again = (
        lax.all_gather(w_qkv, ("fsdp", "ctx"), axis=0, tiled=True),
        lax.all_gather(w_dense, ("fsdp", "ctx"), axis=1, tiled=True),
        lax.all_gather(w_fc1, ("fsdp", "ctx"), axis=0, tiled=True),
        lax.all_gather(w_fc2, ("fsdp", "ctx"), axis=1, tiled=True),
    )
    qkv_flat = again[0].reshape(model_width, 3 * local_cols)
    dense_full, up_full, down_full = (again[1], again[2], again[3])
    grad_out = jnp.concatenate(
        [dy_prompt[0], dy_cont[0].reshape(cont_count * cont_len, model_width)], axis=0
    )
    grad_dense = jnp.dot(attended_low.T, grad_out, preferred_element_type=jnp.float32)
    grad_down = jnp.dot(active_low.T, grad_out, preferred_element_type=jnp.float32)
    grad_shift = jnp.sum(grad_out.astype(jnp.float32), axis=0)
    grad_attended = (
        jnp.dot(grad_out, dense_full.T, preferred_element_type=jnp.float32)
        .astype(jnp.bfloat16)
        .reshape(row_count, head_count, HD)
    )
    scores = masked_scores(
        queries, all_keys, key_limit, query_slot, query_offs, prompt_len, key_slot, key_offs
    )
    probs = jnp.exp(scores - log_total)
    probs_low = probs.astype(jnp.bfloat16)
    grad_probs = jnp.einsum(
        "qhd,khd->hqk", grad_attended, all_values, preferred_element_type=jnp.float32
    )
    inner = jnp.sum(probs * grad_probs, axis=-1, keepdims=True)
    grad_scores = (probs * (grad_probs - inner)).astype(jnp.bfloat16)
    grad_queries = (
        jnp.einsum("hqk,khd->qhd", grad_scores, all_keys, preferred_element_type=jnp.float32)
        * 0.125
    )
    grad_keys = (
        jnp.einsum("hqk,qhd->khd", grad_scores, queries, preferred_element_type=jnp.float32) * 0.125
    )
    grad_values = jnp.einsum(
        "hqk,qhd->khd", probs_low, grad_attended, preferred_element_type=jnp.float32
    )
    prompt_key_grads, prompt_value_grads = (
        lax.psum_scatter(
            grad_keys[:prompt_len].reshape(prompt_len, local_cols),
            "ctx",
            scatter_dimension=0,
            tiled=True,
        ),
        lax.psum_scatter(
            grad_values[:prompt_len].reshape(prompt_len, local_cols),
            "ctx",
            scatter_dimension=0,
            tiled=True,
        ),
    )
    grad_keys = jnp.concatenate(
        [prompt_key_grads.reshape(p_rows, head_count, HD), grad_keys[prompt_len:]], axis=0
    )
    grad_values = jnp.concatenate(
        [prompt_value_grads.reshape(p_rows, head_count, HD), grad_values[prompt_len:]], axis=0
    )
    grad_projected = jnp.stack(
        [rotate(grad_queries, cos_t, -sin_t), rotate(grad_keys, cos_t, -sin_t), grad_values], axis=1
    )
    grad_proj_low = grad_projected.reshape(row_count, 3 * local_cols).astype(jnp.bfloat16)
    grad_qkv = jnp.dot(ln_one.T, grad_proj_low, preferred_element_type=jnp.float32).reshape(
        model_width, 3, local_cols
    )
    grad_qkv_bias = jnp.sum(grad_proj_low.astype(jnp.float32), axis=0).reshape(3, local_cols)
    grad_norm_one = jnp.dot(grad_proj_low, qkv_flat.T, preferred_element_type=jnp.float32)
    grad_active = jnp.dot(grad_out, down_full.T, preferred_element_type=jnp.float32)
    gelu_back = jax.vjp(exact_gelu, hidden)[1]
    grad_hidden_low = gelu_back(grad_active)[0].astype(jnp.bfloat16)
    grad_up = jnp.dot(ln_two.T, grad_hidden_low, preferred_element_type=jnp.float32)
    grad_up_bias = jnp.sum(grad_hidden_low.astype(jnp.float32), axis=0)
    grad_norm_two = jnp.dot(grad_hidden_low, up_full.T, preferred_element_type=jnp.float32)
    norm_back = jax.vjp(norm_pair, inputs, gain_one, shift_one, gain_two, shift_two)[1]
    full_one = lax.psum(grad_norm_one, "tp")
    full_two = lax.psum(grad_norm_two, "tp")
    grad_in, grad_gain_one, grad_shift_one, grad_gain_two, grad_shift_two = norm_back(
        (full_one, full_two)
    )
    grad_inputs = grad_in + grad_out.astype(jnp.float32)
    owned = (
        lax.psum_scatter(grad_qkv, ("fsdp", "ctx"), scatter_dimension=0, tiled=True),
        lax.psum_scatter(grad_dense, ("fsdp", "ctx"), scatter_dimension=1, tiled=True),
        lax.psum_scatter(grad_up, ("fsdp", "ctx"), scatter_dimension=0, tiled=True),
        lax.psum_scatter(grad_down, ("fsdp", "ctx"), scatter_dimension=1, tiled=True),
        lax.psum_scatter(grad_shift, ("fsdp", "ctx"), scatter_dimension=0, tiled=True),
        lax.psum_scatter(grad_gain_one, ("fsdp", "ctx"), scatter_dimension=0, tiled=True),
        lax.psum_scatter(grad_shift_one, ("fsdp", "ctx"), scatter_dimension=0, tiled=True),
        lax.psum_scatter(grad_gain_two, ("fsdp", "ctx"), scatter_dimension=0, tiled=True),
        lax.psum_scatter(grad_shift_two, ("fsdp", "ctx"), scatter_dimension=0, tiled=True),
    )
    bias_qkv_total, bias_up_total = lax.psum((grad_qkv_bias, grad_up_bias), ("fsdp", "ctx"))
    y_prompt = output[:p_rows][None]
    y_cont = output[p_rows:].reshape(1, cont_count, cont_len, model_width)
    dx_prompt = grad_inputs[:p_rows][None]
    dx_cont = grad_inputs[p_rows:].reshape(1, cont_count, cont_len, model_width)
    return (
        y_prompt,
        y_cont,
        dx_prompt,
        dx_cont,
        owned[0],
        bias_qkv_total,
        owned[1],
        owned[4],
        owned[2],
        bias_up_total,
        owned[3],
        owned[4],
        owned[5],
        owned[6],
        owned[7],
        owned[8],
    )


def solution(mesh):
    placed = (
        P("fsdp", "ctx", None),
        P("fsdp", "ctx", None, None),
        P("fsdp", "ctx"),
        P(("fsdp", "ctx"), None, "tp"),
        P(None, "tp"),
        P("tp", ("fsdp", "ctx")),
        P(("fsdp", "ctx")),
        P(("fsdp", "ctx"), "tp"),
        P("tp"),
        P("tp", ("fsdp", "ctx")),
        P(("fsdp", "ctx")),
        P(("fsdp", "ctx")),
        P(("fsdp", "ctx")),
        P(("fsdp", "ctx")),
        P(("fsdp", "ctx")),
        P("fsdp", "ctx", None),
        P("fsdp", "ctx", None, None),
    )
    return jax.shard_map(
        on_device,
        mesh=mesh,
        in_specs=placed,
        out_specs=(
            P("fsdp", "ctx", None),
            P("fsdp", "ctx", None, None),
            P("fsdp", "ctx", None),
            P("fsdp", "ctx", None, None),
            P(("fsdp", "ctx"), None, "tp"),
            P(None, "tp"),
            P("tp", ("fsdp", "ctx")),
            P(("fsdp", "ctx")),
            P(("fsdp", "ctx"), "tp"),
            P("tp"),
            P("tp", ("fsdp", "ctx")),
            P(("fsdp", "ctx")),
            P(("fsdp", "ctx")),
            P(("fsdp", "ctx")),
            P(("fsdp", "ctx")),
            P(("fsdp", "ctx")),
        ),
        check_vma=False,
    )
```

profile of v0, /device:TPU:0, one launch (start us, length us, event | category | flops | bytes accessed | tf_op | source)
XLA Modules:
  0.0 1037.2 jit_solution(66057958732764653)
XLA Ops:
  7.3 1.9 copy.36
  13.8 1.9 convert_reduce_fusion
  15.7 1.7 fusion.19
  18.0 14.7 %all-gather = bf16[8,1,128]{2,1,0:T(2,128)(2,1)S(1)} all-gather(bf16[1,1,128]{2,1,0:T(2,128)(2,1)S(1)} %bitcast.150), channel_id=1, replica_groups=mesh['fsdp'=2,'ctx'=4,'tp'=4] {'fsdp','ctx'}, dimensions={0}, use_global_device_ids=true | all-gather | bytes 2304 | tf_op jit(solution)/shard_map/all_gather | solution.py:84
  32.7 13.2 %all-gather.1 = bf16[8,1,128]{2,1,0:T(2,128)(2,1)S(1)} all-gather(bf16[1,1,128]{2,1,0:T(2,128)(2,1)S(1)} %bitcast.151), channel_id=1, replica_groups=mesh['fsdp'=2,'ctx'=4,'tp'=4] {'fsdp','ctx'}, dimensions={0}, use_global_device_ids=true | all-gather | bytes 2304 | tf_op jit(solution)/shard_map/all_gather | solution.py:85
  48.1 25.5 %all_gather.45 = bf16[256,1024]{1,0:T(8,128)(2,1)S(1)} all-gather(bf16[256,128]{1,0:T(8,128)(2,1)S(1)} %copy-done.22), channel_id=1, replica_groups=mesh['fsdp'=2,'ctx'=4,'tp'=4] {'fsdp','ctx'}, dimensions={1}, use_global_device_ids=true | all-gather | bytes 589824 | tf_op jit(solution)/shard_map/all_gather | solution.py:79
  73.6 12.2 %all-gather.2 = bf16[8,1,128]{2,1,0:T(2,128)(2,1)S(1)} all-gather(bf16[1,1,128]{2,1,0:T(2,128)(2,1)S(1)} %bitcast.153), channel_id=1, replica_groups=mesh['fsdp'=2,'ctx'=4,'tp'=4] {'fsdp','ctx'}, dimensions={0}, use_global_device_ids=true | all-gather | bytes 2304 | tf_op jit(solution)/shard_map/all_gather | solution.py:86
  85.8 13.8 %all-gather.3 = bf16[8,1,128]{2,1,0:T(2,128)(2,1)S(1)} all-gather(bf16[1,1,128]{2,1,0:T(2,128)(2,1)S(1)} %bitcast.154), channel_id=1, replica_groups=mesh['fsdp'=2,'ctx'=4,'tp'=4] {'fsdp','ctx'}, dimensions={0}, use_global_device_ids=true | all-gather | bytes 2304 | tf_op jit(solution)/shard_map/all_gather | solution.py:87
  100.9 2.6 convolution_convert_fusion.2
  103.5 3.9 fusion.2
  107.4 3.6 convolution_add_fusion
  111.9 12.9 %all_gather.44 = bf16[1024,256]{0,1:T(8,128)(2,1)S(1)} all-gather(bf16[256,256]{0,1:T(8,128)(2,1)S(1)} %bitcast.131), channel_id=1, replica_groups=mesh['fsdp'=2,'ctx'=4,'tp'=4] {'ctx'}, dimensions={0}, use_global_device_ids=true | all-gather | bytes 655360 | tf_op jit(solution)/shard_map/all_gather | solution.py:135
  124.8 12.9 %fusion = (f32[4,1024]{1,0:T(4,128)S(1)}, f32[4,1024,1792]{2,1,0:T(8,128)}) fusion(pred[1024,1792]{1,0:T(8,128)(4,1)S(1)} %fusion.2, bf16[1024,4,48]{0,2,1:T(8,128)(2,1)S(1)} %slice.216, bf16[1024,4,16]{0,2,1:T(8,128)(2,1)S(1)} %get-tuple-element.57, bf16[1024,4,64]{0,2,1:T(8,128)(2,1)S(1)} %bitcast.123, bf16[1024,4,48]{0,2,1:T(8,128)(2,1)S(1)} %slice.217, ...), kind=kOutput, calls=%fused_computation.5 | convolution fusion | flops 966717440 | bytes 32784384 | tf_op jit(solution)/shard_map/qhd,khd->hqk/dot_general | solution.py:48
  137.6 13.8 %exponential_reduce_fusion = f32[4,1024]{1,0:T(4,128)S(1)} fusion(f32[4,1024,1792]{2,1,0:T(8,128)} %get-tuple-element.66, f32[4,1024]{1,0:T(4,128)S(1)} %get-tuple-element.65, pred[1024,1792]{1,0:T(8,128)(4,1)S(1)} %fusion.2), kind=kLoop, calls=%fused_computation.3 | loop fusion | flops 29356032 | bytes 31227904 | tf_op jit(solution)/shard_map/reduce_sum | solution.py:148
  151.4 12.7 %all_gather.43 = bf16[1024,256]{0,1:T(8,128)(2,1)S(1)} all-gather(bf16[256,256]{0,1:T(8,128)(2,1)S(1)} %bitcast.132), channel_id=1, replica_groups=mesh['fsdp'=2,'ctx'=4,'tp'=4] {'ctx'}, dimensions={0}, use_global_device_ids=true | all-gather | bytes 655360 | tf_op jit(solution)/shard_map/all_gather | solution.py:136
  164.2 22.0 %multiply_reduce_fusion = (f32[4,1024]{1,0:T(4,128)S(1)}, f32[4,1024,1792]{2,1,0:T(8,128)}) fusion(f32[4,1024,1792]{2,1,0:T(8,128)} %get-tuple-element.66, f32[4,1024]{1,0:T(4,128)S(1)} %log_add_fusion, pred[1024,1792]{1,0:T(8,128)(4,1)S(1)} %fusion.2, bf16[1024,4,64]{0,2,1:T(8,128)(2,1)S(1)} %bitcast.129, bf16[768,4,64]{0,2,1:T(8,128)(2,1)S(1)} %slice_bitcast_fusion.4, ...), kind=kOutput, calls=%fused_computation.1 | convolution fusion | flops 978055168 | bytes 62029824 | tf_op jit(solution)/shard_map/qhd,khd->hqk/dot_general | solution.py:186
  186.2 24.6 %multiply_convert_fusion = bf16[4,1024,1792]{2,1,0:T(8,128)(2,1)} fusion(f32[4,1024,1792]{2,1,0:T(8,128)} %get-tuple-element.69, f32[4,1024,1792]{2,1,0:T(8,128)} %get-tuple-element.66, f32[4,1024]{1,0:T(4,128)S(1)} %get-tuple-element.68, f32[4,1024]{1,0:T(4,128)S(1)} %log_add_fusion, pred[1024,1792]{1,0:T(8,128)(4,1)S(1)} %fusion.2), kind=kLoop, calls=%fused_computation | loop fusion | flops 44040192 | bytes 75268096 | tf_op jit(solution)/shard_map/convert_element_type | solution.py:190
  210.8 7.8 fusion.30
  220.7 12.7 %convolution_bitcast_fusion = f32[1792,4,64]{0,2,1:T(8,128)S(1)} fusion(bf16[1024,4,64]{0,2,1:T(8,128)(2,1)S(1)} %bitcast.130, f32[4,1024,1792]{2,1,0:T(8,128)} %get-tuple-element.66, f32[4,1024]{1,0:T(4,128)S(1)} %log_add_fusion, pred[1024,1792]{1,0:T(8,128)(4,1)S(1)} %fusion.2), kind=kOutput, calls=%fused_computation.58 | convolution fusion | flops 968884224 | bytes 33570816 | tf_op jit(solution)/shard_map/hqk,qhd->khd/dot_general | solution.py:198
  235.3 9.7 fusion.35
  246.9 14.3 %convolution_convert_fusion.1 = bf16[4,64,1024]{2,1,0:T(8,128)(2,1)} fusion(bf16[768,4,64]{0,2,1:T(8,128)(2,1)} %copy-done.13, bf16[1024,4,64]{0,2,1:T(8,128)(2,1)} %bitcast.117, f32[4,1024,1792]{2,1,0:T(8,128)} %get-tuple-element.66, f32[4,1024]{1,0:T(4,128)S(1)} %log_add_fusion, pred[1024,1792]{1,0:T(8,128)(4,1)S(1)} %fusion.2), kind=kOutput, calls=%fused_computation.75 | convolution fusion | flops 970981376 | bytes 32653312 | tf_op jit(solution)/shard_map/hqk,khd->qhd/dot_general | solution.py:150
  261.2 4.0 fusion.78
  265.5 16.0 %multiply_convert_fusion.1 = (bf16[1024,1024]{1,0:T(8,128)(2,1)}, f32[1024,1024]{1,0:T(8,128)}, f32[1024,1024]{1,0:T(8,128)}) fusion(f32[1024]{0:T(1024)S(1)} %copy-done.26, bf16[1024,1024]{1,0:T(8,128)(2,1)} %all-gather.12.cloned.1.call-done, f32[1024]{0:T(1024)S(1)} %bitcast.148, f32[1024]{0:T(1024)S(1)} %bitcast.139, f32[1024]{0:T(1024)S(1)} %fusion.55, ...), kind=kOutput, calls=%fused_computation.41 | convolution fusion | flops 2226126848 | bytes 14700544 | tf_op jit(solution)/shard_map/dot_general | solution.py:153
  281.5 9.1 convert_reduce_fusion.2
  292.0 4.4 fusion.79
  298.3 1.8 fusion.38
  300.2 5.3 reduce-scatter.9.cloned.1.call-done
  306.7 1.3 convert_reduce_fusion.3
  309.2 3.8 fusion.80
  313.4 6.0 convolution_convert_fusion
  319.5 3.3 fusion.73
  322.8 5.3 fusion.31
  328.2 6.2 fusion.64
  334.5 6.4 fusion.72
  341.5 13.7 %all-gather.4 = bf16[8,1,128]{2,1,0:T(2,128)(2,1)S(1)} all-gather(bf16[1,1,128]{2,1,0:T(2,128)(2,1)S(1)} %bitcast.155), channel_id=1, replica_groups=mesh['fsdp'=2,'ctx'=4,'tp'=4] {'fsdp','ctx'}, dimensions={0}, use_global_device_ids=true | all-gather | bytes 2304 | tf_op jit(solution)/shard_map/all_gather | solution.py:82
  355.2 13.4 %all-gather.5 = bf16[8,1,128]{2,1,0:T(2,128)(2,1)S(1)} all-gather(bf16[1,1,128]{2,1,0:T(2,128)(2,1)S(1)} %bitcast.156), channel_id=1, replica_groups=mesh['fsdp'=2,'ctx'=4,'tp'=4] {'fsdp','ctx'}, dimensions={0}, use_global_device_ids=true | all-gather | bytes 2304 | tf_op jit(solution)/shard_map/all_gather | solution.py:83
  369.8 370.8 %all-reduce.16.cloned.1.call-done = (f32[1024,1024]{1,0:T(8,128)}, f32[1024,1024]{1,0:T(8,128)}, f32[1024,1024]{1,0:T(8,128)}) async-done(((f32[1024,1024]{1,0:T(8,128)}, f32[1024,1024]{1,0:T(8,128)}, f32[1024,1024]{1,0:T(8,128)}), (f32[1024,1024]{1,0:T(8,128)}, f32[1024,1024]{1,0:T(8,128)}, f32[1024,1024]{1,0:T(8,128)})) %all-reduce.16.cloned.1.call-update) | async-done | bytes 12582928 | tf_op jit(solution)/shard_map/psum | solution.py:158
  740.7 4.7 fusion.76
  745.4 83.7 %all-reduce.14.cloned.1.call-done = bf16[1024,1024]{1,0:T(8,128)(2,1)} async-done(((bf16[1024,1024]{1,0:T(8,128)(2,1)}), bf16[1024,1024]{1,0:T(8,128)(2,1)}) %all-reduce.14.cloned.1.call-update) | async-done | bytes 2097168 | tf_op jit(solution)/shard_map/psum | solution.py:159
  829.1 9.3 fusion.18
  838.4 5.4 convert_reduce_fusion.1
  843.8 26.6 %all-reduce.9 = (f32[3,256]{1,0:T(4,128)}, f32[1024]{0:T(1024)S(1)}, f32[1024]{0:T(1024)}, f32[1024]{0:T(1024)S(1)}, f32[1024]{0:T(1024)S(1)}, /*index=5*/f32[1024]{0:T(1024)S(1)}, f32[1024]{0:T(1024)S(1)}) all-reduce(f32[3,256]{1,0:T(4,128)S(1)} %reshape.336, ...), channel_id=1, replica_groups=mesh['fsdp'=2,'ctx'=4,'tp'=4] {'fsdp','ctx'}, use_global_device_ids=true, to_apply=%region_17.18 | all-reduce | flops 6912 | bytes 55296 | tf_op jit(solution)/shard_map/psum | solution.py:254
  872.8 4.0 slice.168
  876.8 1.9 slice.152
  878.7 2.3 slice_bitcast_fusion
  882.0 36.9 %reduce-scatter.11.cloned.1.call-done = f32[128,3,256]{2,0,1:T(8,128)} async-done(((f32[1024,3,256]{2,0,1:T(8,128)}), f32[128,3,256]{2,0,1:T(8,128)}) %reduce-scatter.11.cloned.1.call-update) | async-done | bytes 393232 | tf_op jit(solution)/shard_map/reduce_scatter | solution.py:244
  919.0 55.1 %reduce-scatter.15.cloned.1.call-done = f32[128,1024]{1,0:T(8,128)} async-done(((f32[1024,1024]{1,0:T(8,128)}), f32[128,1024]{1,0:T(8,128)}) %reduce-scatter.15.cloned.1.call-update) | async-done | bytes 524304 | tf_op jit(solution)/shard_map/reduce_scatter | solution.py:246
  974.1 55.6 %reduce-scatter.17.cloned.1.call-done = f32[1024,128]{1,0:T(8,128)} async-done(((f32[1024,1024]{1,0:T(8,128)}), f32[1024,128]{1,0:T(8,128)}) %reduce-scatter.17.cloned.1.call-update) | async-done | bytes 524304 | tf_op jit(solution)/shard_map/reduce_scatter | solution.py:247
  (176 shorter events, 27.1 us)
Async XLA Ops:
  7.2 8.5 copy-start
  7.2 10.8 %copy-start.32 = (bf16[128]{0:T(256)(128)(2,1)S(1)}, bf16[128]{0:T(256)(128)(2,1)}, u32[]{:S(2)}) copy-start(bf16[128]{0:T(256)(128)(2,1)} %param.28) | copy-start | bytes 772
  7.2 25.5 %copy-start.33 = (bf16[128]{0:T(256)(128)(2,1)S(1)}, bf16[128]{0:T(256)(128)(2,1)}, u32[]{:S(2)}) copy-start(bf16[128]{0:T(256)(128)(2,1)} %param.29) | copy-start | bytes 772
  7.2 39.3 %copy-start.30 = (bf16[3,256]{1,0:T(4,128)(2,1)S(1)}, bf16[3,256]{1,0:T(4,128)(2,1)}, u32[]{:S(2)}) copy-start(bf16[3,256]{1,0:T(4,128)(2,1)} %param.21) | copy-start | bytes 4612
  7.2 39.9 %copy-start.34 = (s32[1,3]{1,0:T(1,128)S(1)}, s32[1,3]{1,0:T(1,128)}, u32[]{:S(2)}) copy-start(s32[1,3]{1,0:T(1,128)} %param.19) | copy-start | bytes 40
  7.2 40.9 %copy-start.22 = (bf16[256,128]{1,0:T(8,128)(2,1)S(1)}, bf16[256,128]{1,0:T(8,128)(2,1)}, u32[]{:S(2)}) copy-start(bf16[256,128]{1,0:T(8,128)(2,1)} %param.22) | copy-start | bytes 196612
  7.2 66.3 %copy-start.35 = (bf16[128]{0:T(256)(128)(2,1)S(1)}, bf16[128]{0:T(256)(128)(2,1)}, u32[]{:S(2)}) copy-start(bf16[128]{0:T(256)(128)(2,1)} %param.30) | copy-start | bytes 772
  7.3 78.6 %copy-start.36 = (bf16[128]{0:T(256)(128)(2,1)S(1)}, bf16[128]{0:T(256)(128)(2,1)}, u32[]{:S(2)}) copy-start(bf16[128]{0:T(256)(128)(2,1)} %param.31) | copy-start | bytes 772
  7.3 93.0 %copy-start.31 = (bf16[1024]{0:T(1024)(128)(2,1)S(1)}, bf16[1024]{0:T(1024)(128)(2,1)}, u32[]{:S(2)}) copy-start(bf16[1024]{0:T(1024)(128)(2,1)} %param.25) | copy-start | bytes 6148
  7.3 93.6 %copy-start.6 = (bf16[1,3,256,1024]{3,2,1,0:T(8,128)(2,1)S(1)}, bf16[1,3,256,1024]{3,2,1,0:T(8,128)(2,1)}, u32[]{:S(2)}) copy-start(bf16[1,3,256,1024]{3,2,1,0:T(8,128)(2,1)} %param.33) | copy-start | bytes 4718596
  7.3 100.1 %all-gather.10.cloned.1.call-start = ((), (), s32[]{:S(2)}) async-start(), calls=%async_computation.6 | async-start | bytes 1769472 | tf_op jit(solution)/shard_map/all_gather | solution.py:78
  9.2 256.2 %all-gather.12.cloned.1.call-start = ((), (), s32[]{:S(2)}) async-start(), calls=%async_computation.7 | async-start | bytes 2359296 | tf_op jit(solution)/shard_map/all_gather | solution.py:80
  10.0 271.5 %all-gather.14.cloned.1.call-start = ((), (), s32[]{:S(2)}) async-start(), calls=%async_computation.8 | async-start | bytes 2359296 | tf_op jit(solution)/shard_map/all_gather | solution.py:81
  10.7 285.6 %reduce-scatter.7.cloned.1.call-start = ((), (), s32[]{:S(2)}) async-start(), calls=%async_computation.10 | async-start | bytes 1310720 | tf_op jit(solution)/shard_map/reduce_scatter | solution.py:202
  32.7 74.7 %copy-start.20 = (f32[8,1,128]{2,1,0:T(1,128)}, f32[8,1,128]{2,1,0:T(1,128)S(1)}, u32[]{:S(2)}) copy-start(f32[8,1,128]{2,1,0:T(1,128)S(1)} %convert_element_type.144) | copy-start | bytes 12292
  48.1 63.7 %copy-start.16 = (f32[1024,16]{0,1:T(8,128)}, f32[1024,16]{0,1:T(8,128)S(1)}, u32[]{:S(2)}) copy-start(f32[1024,16]{0,1:T(8,128)S(1)} %pad_maximum_fusion.9) | copy-start | bytes 196612
  73.6 29.9 %copy-start.11 = (bf16[256,1024]{1,0:T(8,128)(2,1)}, bf16[256,1024]{1,0:T(8,128)(2,1)S(1)}, u32[]{:S(2)}) copy-start(bf16[256,1024]{1,0:T(8,128)(2,1)S(1)} %all_gather.45) | copy-start | bytes 1572868
  111.7 52.4 %copy-start.13 = (bf16[768,4,64]{0,2,1:T(8,128)(2,1)}, bf16[768,4,64]{0,2,1:T(8,128)(2,1)S(1)}, u32[]{:S(2)}) copy-start(bf16[768,4,64]{0,2,1:T(8,128)(2,1)S(1)} %slice_bitcast_fusion.4) | copy-start | bytes 1179652
  137.6 26.6 %copy-start.18 = (bf16[1024,256]{0,1:T(8,128)(2,1)S(1)}, bf16[1024,256]{0,1:T(8,128)(2,1)}, u32[]{:S(2)}) copy-start(bf16[1024,256]{0,1:T(8,128)(2,1)} %convolution_convert_fusion.2) | copy-start | bytes 1572868
  164.2 22.0 %copy-start.9 = (bf16[1024,256]{0,1:T(8,128)(2,1)}, bf16[1024,256]{0,1:T(8,128)(2,1)S(1)}, u32[]{:S(2)}) copy-start(bf16[1024,256]{0,1:T(8,128)(2,1)S(1)} %all_gather.43) | copy-start | bytes 1572868
  246.8 58.7 %reduce-scatter.9.cloned.1.call-start = ((), (), s32[]{:S(2)}) async-start(), calls=%async_computation.11 | async-start | bytes 1310720 | tf_op jit(solution)/shard_map/reduce_scatter | solution.py:208
  261.2 4.2 copy-start.4
  261.2 4.2 copy-start.26
  261.2 4.3 copy-start.28
  265.2 475.5 %all-reduce.16.cloned.1.call-start = ((), (), s32[]{:S(2)}) async-start(), calls=%async_computation.16 | async-start | bytes 25165824 | tf_op jit(solution)/shard_map/psum | solution.py:158
  265.5 16.0 %copy-start.10 = (bf16[1,256,1024]{2,1,0:T(8,128)(2,1)S(1)}, bf16[1,256,1024]{2,1,0:T(8,128)(2,1)}, u32[]{:S(2)}) copy-start(bf16[1,256,1024]{2,1,0:T(8,128)(2,1)} %param.32) | copy-start | bytes 1572868
  281.5 10.4 %copy-start.39 = (bf16[1024,1024]{1,0:T(8,128)(2,1)S(1)}, bf16[1024,1024]{1,0:T(8,128)(2,1)}, u32[]{:S(2)}) copy-start(bf16[1024,1024]{1,0:T(8,128)(2,1)} %all-gather.12.cloned.1.call-done) | copy-start | bytes 6291460
  291.9 4.4 copy-start.5
  291.9 5.2 copy-start.17
  291.9 5.2 copy-start.19
  296.3 3.8 copy-start.14
  305.5 3.7 copy-start.40
  313.1 516.0 %all-reduce.14.cloned.1.call-start = ((), (), s32[]{:S(2)}) async-start(), calls=%async_computation.9 | async-start | bytes 4194304 | tf_op jit(solution)/shard_map/psum | solution.py:159
  313.3 6.1 copy-start.12
  319.4 562.6 %reduce-scatter.13.cloned.1.call-start = ((), (), s32[]{:S(2)}) async-start(), calls=%async_computation.13 | async-start | bytes 1179648 | tf_op jit(solution)/shard_map/reduce_scatter | solution.py:245
  322.7 596.2 %reduce-scatter.11.cloned.1.call-start = ((), (), s32[]{:S(2)}) async-start(), calls=%async_computation.12 | async-start | bytes 3538944 | tf_op jit(solution)/shard_map/reduce_scatter | solution.py:244
  322.8 5.4 copy-start.29
  328.1 646.0 %reduce-scatter.15.cloned.1.call-start = ((), (), s32[]{:S(2)}) async-start(), calls=%async_computation.14 | async-start | bytes 4718592 | tf_op jit(solution)/shard_map/reduce_scatter | solution.py:246
  334.4 695.3 %reduce-scatter.17.cloned.1.call-start = ((), (), s32[]{:S(2)}) async-start(), calls=%async_computation.15 | async-start | bytes 4718592 | tf_op jit(solution)/shard_map/reduce_scatter | solution.py:247
  340.8 14.3 %copy-start.38 = (bf16[128]{0:T(256)(128)(2,1)S(1)}, bf16[128]{0:T(256)(128)(2,1)}, u32[]{:S(2)}) copy-start(bf16[128]{0:T(256)(128)(2,1)} %param.27) | copy-start | bytes 772
  340.8 27.7 %copy-start.41 = (u32[32]{0:T(128)S(1)}, u32[32]{0:T(128)}, u32[]{:S(2)}) copy-start(u32[32]{0:T(128)} %constant.122) | copy-start | bytes 388
  740.7 4.7 copy-start.24
  829.1 9.3 copy-start.1
  829.1 9.3 copy-start.2
  829.1 9.3 copy-start.7
  838.4 5.4 copy-start.25
  870.4 6.4 copy-start.3
  870.5 159.3 %copy-start.42 = (f32[128]{0:T(128)}, f32[128]{0:T(128)S(1)}, u32[]{:S(2)}) copy-start(f32[128]{0:T(128)S(1)} %dynamic-slice.1) | copy-start | bytes 1540
  (7 other events, 11.7 us)
Sparse Core Ops, SparseCore 0:
  10.6 28.5 all-gather.9
  41.1 33.7 all-gather.11
  76.8 28.1 all-gather.13
  246.9 27.1 reduce-scatter.6
  277.7 27.7 reduce-scatter.8
  313.2 427.4 all-reduce.15
  743.6 85.4 all-reduce.13
  833.1 35.1 reduce-scatter.12
  872.7 46.2 reduce-scatter.10
  922.7 51.3 reduce-scatter.14
  978.4 51.2 reduce-scatter.16
where the time goes:
time: 1050 us; the launch traced here: 1040 us
  waiting for transfers between devices  609 us (58%)
  blocking collectives  159 us (15%)
  matrix products  150 us (14%)
  other arithmetic  76 us (7%)
  local copies, waits for them, and re-layouts  27.1 us (3%)
  between operations  15.5 us (1%)
    psum x1, waiting for transfers between devices, on_device(): attn_total = lax.psum(attn_part, 'tp')  371 us
    psum x1, waiting for transfers between devices, on_device(): lax.psum(mlp_part.astype(jnp.bfloat16), 'tp').astype(jnp.float32)  83.7 us
    reduce_scatter x1, waiting for transfers between devices, on_device(): lax.psum_scatter(grad_down, ('fsdp', 'ctx'), scatter_dimension=1, tiled=T...  55.6 us
    reduce_scatter x1, waiting for transfers between devices, on_device(): lax.psum_scatter(grad_up, ('fsdp', 'ctx'), scatter_dimension=0, tiled=True)  55.1 us
    reduce_scatter x1, waiting for transfers between devices, on_device(): lax.psum_scatter(grad_qkv, ('fsdp', 'ctx'), scatter_dimension=0, tiled=True)  36.9 us
    psum x1, blocking collectives, on_device(): lax.psum((grad_qkv_bias, grad_up_bias), ('fsdp', 'ctx'))  26.6 us
    all_gather x1, blocking collectives, on_device(): lax.all_gather(w_dense, ('fsdp', 'ctx'), axis=1, tiled=True)  25.5 us
    convert_element_type x1, other arithmetic, on_device(): grad_scores = (probs * (grad_probs - inner)).astype(jnp.bfloat16)  24.6 us
  transfers between devices with their start and end apart: 11, of which 6 were waited for; matrix products, arithmetic and copies ran while one was open for 23% of the time, Pallas kernels for 0%

commit v1 on v0

--- a/solution.py
+++ b/solution.py
@@ -155,7 +155,11 @@
     )
     active_low = exact_gelu(hidden).astype(jnp.bfloat16)
     mlp_part = jnp.dot(active_low, down_full, preferred_element_type=jnp.float32)
-    attn_total = lax.psum(attn_part, "tp")
+    attn_total = attn_part
+    for hop in (1, 2):
+        attn_total = attn_total + lax.ppermute(
+            attn_total, "tp", [(dev, dev ^ hop) for dev in range(4)]
+        )
     mlp_total = lax.psum(mlp_part.astype(jnp.bfloat16), "tp").astype(jnp.float32)
     mixed = attn_total + mlp_total
     output = inputs + mixed + dense_shift + down_shift

time: 1050 us -> 1140 us (1.086)
  waiting for transfers between devices: 609 us -> 699 us
    ppermute x0 -> x2, waiting for transfers between devices: none -> 193 us  [on_device(): lax.ppermute(attn_total, 'tp', [(dev, dev ^ hop) for dev in range(4)])]
    psum x1, waiting for transfers between devices: 371 us -> 264 us  [on_device(): full_two = lax.psum(grad_norm_two, 'tp')]
    psum x1, waiting for transfers between devices: 83.7 us -> 95.1 us  [on_device(): lax.psum(mlp_part.astype(jnp.bfloat16), 'tp').astype(jnp.float32)]
  transfers between devices with their start and end apart: 11 -> 13, of which waited for: 6 -> 6; matrix products, arithmetic and copies ran while one was open for 23% -> 21% of each run, Pallas kernels for 0% -> 0%
where the time goes in v1:
time: 1140 us; the launch traced here: 1130 us
  waiting for transfers between devices  699 us (61%)
  blocking collectives  158 us (14%)
  matrix products  146 us (13%)
  other arithmetic  80.6 us (7%)
  local copies, waits for them, and re-layouts  25 us (2%)
  between operations  15.4 us (1%)
    psum x1, waiting for transfers between devices, on_device(): full_two = lax.psum(grad_norm_two, 'tp')  264 us
    ppermute x2, waiting for transfers between devices, on_device(): lax.ppermute(attn_total, 'tp', [(dev, dev ^ hop) for dev in range(4)])  193 us
    psum x1, waiting for transfers between devices, on_device(): lax.psum(mlp_part.astype(jnp.bfloat16), 'tp').astype(jnp.float32)  95.1 us
    reduce_scatter x1, waiting for transfers between devices, on_device(): lax.psum_scatter(grad_down, ('fsdp', 'ctx'), scatter_dimension=1, tiled=T...  55.6 us
    reduce_scatter x1, waiting for transfers between devices, on_device(): lax.psum_scatter(grad_up, ('fsdp', 'ctx'), scatter_dimension=0, tiled=True)  55.1 us
    reduce_scatter x1, waiting for transfers between devices, on_device(): lax.psum_scatter(grad_qkv, ('fsdp', 'ctx'), scatter_dimension=0, tiled=True)  35.6 us
    psum x1, blocking collectives, on_device(): lax.psum((grad_qkv_bias, grad_up_bias), ('fsdp', 'ctx'))  26.7 us
    convert_element_type x1, other arithmetic, on_device(): grad_scores = (probs * (grad_probs - inner)).astype(jnp.bfloat16)  24.7 us
  transfers between devices with their start and end apart: 13, of which 6 were waited for; matrix products, arithmetic and copies ran while one was open for 21% of the time, Pallas kernels for 0%

profile of v1, /device:TPU:0, one launch (start us, length us, event | category | flops | bytes accessed | tf_op | source)
XLA Modules:
  0.0 1127.7 jit_solution(9808546402431840037)
XLA Ops:
  7.3 1.9 copy.36
  10.9 1.9 convert_reduce_fusion
  12.8 1.7 fusion.19
  14.6 14.7 %all-gather = bf16[8,1,128]{2,1,0:T(2,128)(2,1)S(1)} all-gather(bf16[1,1,128]{2,1,0:T(2,128)(2,1)S(1)} %bitcast.150), channel_id=1, replica_groups=mesh['fsdp'=2,'ctx'=4,'tp'=4] {'fsdp','ctx'}, dimensions={0}, use_global_device_ids=true | all-gather | bytes 2304 | tf_op jit(solution)/shard_map/all_gather | solution.py:84
  29.3 13.2 %all-gather.1 = bf16[8,1,128]{2,1,0:T(2,128)(2,1)S(1)} all-gather(bf16[1,1,128]{2,1,0:T(2,128)(2,1)S(1)} %bitcast.151), channel_id=1, replica_groups=mesh['fsdp'=2,'ctx'=4,'tp'=4] {'fsdp','ctx'}, dimensions={0}, use_global_device_ids=true | all-gather | bytes 2304 | tf_op jit(solution)/shard_map/all_gather | solution.py:85
  44.1 24.6 %all_gather.45 = bf16[256,1024]{1,0:T(8,128)(2,1)S(1)} all-gather(bf16[256,128]{1,0:T(8,128)(2,1)S(1)} %copy-done.29), channel_id=1, replica_groups=mesh['fsdp'=2,'ctx'=4,'tp'=4] {'fsdp','ctx'}, dimensions={1}, use_global_device_ids=true | all-gather | bytes 589824 | tf_op jit(solution)/shard_map/all_gather | solution.py:79
  68.7 12.5 %all-gather.2 = bf16[8,1,128]{2,1,0:T(2,128)(2,1)S(1)} all-gather(bf16[1,1,128]{2,1,0:T(2,128)(2,1)S(1)} %bitcast.153), channel_id=1, replica_groups=mesh['fsdp'=2,'ctx'=4,'tp'=4] {'fsdp','ctx'}, dimensions={0}, use_global_device_ids=true | all-gather | bytes 2304 | tf_op jit(solution)/shard_map/all_gather | solution.py:86
  81.9 13.9 %all-gather.3 = bf16[8,1,128]{2,1,0:T(2,128)(2,1)S(1)} all-gather(bf16[1,1,128]{2,1,0:T(2,128)(2,1)S(1)} %bitcast.154), channel_id=1, replica_groups=mesh['fsdp'=2,'ctx'=4,'tp'=4] {'fsdp','ctx'}, dimensions={0}, use_global_device_ids=true | all-gather | bytes 2304 | tf_op jit(solution)/shard_map/all_gather | solution.py:87
  97.0 2.6 convolution_convert_fusion.2
  99.5 3.0 fusion.2
  102.6 3.6 convolution_add_fusion
  107.5 13.0 %all_gather.44 = bf16[1024,256]{0,1:T(8,128)(2,1)S(1)} all-gather(bf16[256,256]{0,1:T(8,128)(2,1)S(1)} %bitcast.131), channel_id=1, replica_groups=mesh['fsdp'=2,'ctx'=4,'tp'=4] {'ctx'}, dimensions={0}, use_global_device_ids=true | all-gather | bytes 655360 | tf_op jit(solution)/shard_map/all_gather | solution.py:135
  120.5 12.9 %fusion = (f32[4,1024]{1,0:T(4,128)S(1)}, f32[4,1024,1792]{2,1,0:T(8,128)}) fusion(pred[1024,1792]{1,0:T(8,128)(4,1)S(1)} %fusion.2, bf16[1024,4,48]{0,2,1:T(8,128)(2,1)S(1)} %slice.216, bf16[1024,4,16]{0,2,1:T(8,128)(2,1)S(1)} %get-tuple-element.56, bf16[1024,4,64]{0,2,1:T(8,128)(2,1)S(1)} %bitcast.123, bf16[1024,4,48]{0,2,1:T(8,128)(2,1)S(1)} %slice.217, ...), kind=kOutput, calls=%fused_computation.5 | convolution fusion | flops 966717440 | bytes 32784384 | tf_op jit(solution)/shard_map/qhd,khd->hqk/dot_general | solution.py:48
  133.3 13.8 %exponential_reduce_fusion = f32[4,1024]{1,0:T(4,128)S(1)} fusion(f32[4,1024,1792]{2,1,0:T(8,128)} %get-tuple-element.66, f32[4,1024]{1,0:T(4,128)S(1)} %get-tuple-element.65, pred[1024,1792]{1,0:T(8,128)(4,1)S(1)} %fusion.2), kind=kLoop, calls=%fused_computation.3 | loop fusion | flops 29356032 | bytes 31227904 | tf_op jit(solution)/shard_map/reduce_sum | solution.py:148
  147.1 12.7 %all_gather.43 = bf16[1024,256]{0,1:T(8,128)(2,1)S(1)} all-gather(bf16[256,256]{0,1:T(8,128)(2,1)S(1)} %bitcast.132), channel_id=1, replica_groups=mesh['fsdp'=2,'ctx'=4,'tp'=4] {'ctx'}, dimensions={0}, use_global_device_ids=true | all-gather | bytes 655360 | tf_op jit(solution)/shard_map/all_gather | solution.py:136
  159.8 22.0 %multiply_reduce_fusion = (f32[4,1024]{1,0:T(4,128)S(1)}, f32[4,1024,1792]{2,1,0:T(8,128)}) fusion(f32[4,1024,1792]{2,1,0:T(8,128)} %get-tuple-element.66, f32[4,1024]{1,0:T(4,128)S(1)} %log_add_fusion, pred[1024,1792]{1,0:T(8,128)(4,1)S(1)} %fusion.2, bf16[1024,4,64]{0,2,1:T(8,128)(2,1)S(1)} %bitcast.130, bf16[768,4,64]{0,2,1:T(8,128)(2,1)S(1)} %slice_bitcast_fusion.4, ...), kind=kOutput, calls=%fused_computation.1 | convolution fusion | flops 978055168 | bytes 62029824 | tf_op jit(solution)/shard_map/qhd,khd->hqk/dot_general | solution.py:190
  181.8 24.7 %multiply_convert_fusion = bf16[4,1024,1792]{2,1,0:T(8,128)(2,1)} fusion(f32[4,1024,1792]{2,1,0:T(8,128)} %get-tuple-element.68, f32[4,1024,1792]{2,1,0:T(8,128)} %get-tuple-element.66, f32[4,1024]{1,0:T(4,128)S(1)} %get-tuple-element.67, f32[4,1024]{1,0:T(4,128)S(1)} %log_add_fusion, pred[1024,1792]{1,0:T(8,128)(4,1)S(1)} %fusion.2), kind=kLoop, calls=%fused_computation | loop fusion | flops 44040192 | bytes 75268096 | tf_op jit(solution)/shard_map/convert_element_type | solution.py:194
  206.5 7.8 fusion.30
  216.5 14.0 %convolution_bitcast_fusion = f32[1792,4,64]{0,2,1:T(8,128)S(1)} fusion(bf16[1024,4,64]{0,2,1:T(8,128)(2,1)} %bitcast.129, f32[4,1024,1792]{2,1,0:T(8,128)} %get-tuple-element.66, f32[4,1024]{1,0:T(4,128)S(1)} %log_add_fusion, pred[1024,1792]{1,0:T(8,128)(4,1)S(1)} %fusion.2), kind=kOutput, calls=%fused_computation.58 | convolution fusion | flops 968884224 | bytes 33570816 | tf_op jit(solution)/shard_map/hqk,qhd->khd/dot_general | solution.py:202
  232.3 9.7 fusion.35
  244.2 15.7 %multiply_convert_fusion.1 = (bf16[1024,1024]{1,0:T(8,128)(2,1)}, f32[1024,1024]{1,0:T(8,128)}, f32[1024,1024]{1,0:T(8,128)}) fusion(f32[1024]{0:T(1024)} %convert_element_type.129, bf16[1024,1024]{1,0:T(8,128)(2,1)} %all-gather.12.cloned.1.call-done, f32[1024]{0:T(1024)} %bitcast.148, f32[1024]{0:T(1024)} %bitcast.139, f32[1024]{0:T(1024)} %copy-done.35, ...), kind=kOutput, calls=%fused_computation.41 | convolution fusion | flops 2226126848 | bytes 14700544 | tf_op jit(solution)/shard_map/dot_general | solution.py:153
  259.9 9.2 convert_reduce_fusion.2
  270.4 4.3 fusion.79
  277.0 2.1 fusion.38
  283.8 3.8 fusion.80
  288.1 5.9 convolution_convert_fusion
  294.0 14.2 %convolution_convert_fusion.1 = bf16[4,64,1024]{2,1,0:T(8,128)(2,1)} fusion(bf16[768,4,64]{0,2,1:T(8,128)(2,1)} %copy-done.19, bf16[1024,4,64]{0,2,1:T(8,128)(2,1)} %bitcast.117, f32[4,1024,1792]{2,1,0:T(8,128)} %get-tuple-element.66, f32[4,1024]{1,0:T(4,128)S(1)} %log_add_fusion, pred[1024,1792]{1,0:T(8,128)(4,1)S(1)} %fusion.2), kind=kOutput, calls=%fused_computation.75 | convolution fusion | flops 970981376 | bytes 32653312 | tf_op jit(solution)/shard_map/hqk,khd->qhd/dot_general | solution.py:150
  308.3 3.5 fusion.73
  311.9 5.3 fusion.31
  317.3 6.2 fusion.64
  325.4 1.8 collective-permute-start
  327.2 192.7 %collective-permute-done = f32[1024,1024]{1,0:T(8,128)S(1)} collective-permute-done((f32[1024,1024]{1,0:T(8,128)S(1)}, f32[1024,1024]{1,0:T(8,128)S(1)}, u32[]{:S(2)}, u32[]{:S(2)}) %collective-permute-start) | collective-permute-done | bytes 4194336 | tf_op jit(solution)/shard_map/ppermute | solution.py:160
  519.9 2.9 add.177
  523.2 4.5 fusion.72
  528.4 13.6 %all-gather.4 = bf16[8,1,128]{2,1,0:T(2,128)(2,1)S(1)} all-gather(bf16[1,1,128]{2,1,0:T(2,128)(2,1)S(1)} %bitcast.155), channel_id=1, replica_groups=mesh['fsdp'=2,'ctx'=4,'tp'=4] {'fsdp','ctx'}, dimensions={0}, use_global_device_ids=true | all-gather | bytes 2304 | tf_op jit(solution)/shard_map/all_gather | solution.py:82
  541.9 13.1 %all-gather.5 = bf16[8,1,128]{2,1,0:T(2,128)(2,1)S(1)} all-gather(bf16[1,1,128]{2,1,0:T(2,128)(2,1)S(1)} %bitcast.156), channel_id=1, replica_groups=mesh['fsdp'=2,'ctx'=4,'tp'=4] {'fsdp','ctx'}, dimensions={0}, use_global_device_ids=true | all-gather | bytes 2304 | tf_op jit(solution)/shard_map/all_gather | solution.py:83
  556.4 263.6 %all-reduce.16.cloned.1.call-done = (f32[1024,1024]{1,0:T(8,128)}, f32[1024,1024]{1,0:T(8,128)}) async-done(((f32[1024,1024]{1,0:T(8,128)}, f32[1024,1024]{1,0:T(8,128)}), (f32[1024,1024]{1,0:T(8,128)}, f32[1024,1024]{1,0:T(8,128)})) %all-reduce.16.cloned.1.call-update) | async-done | bytes 8388624 | tf_op jit(solution)/shard_map/psum | solution.py:242
  820.0 4.7 fusion.76
  824.7 95.1 %all-reduce.14.cloned.1.call-done = bf16[1024,1024]{1,0:T(8,128)(2,1)} async-done(((bf16[1024,1024]{1,0:T(8,128)(2,1)}), bf16[1024,1024]{1,0:T(8,128)(2,1)}) %all-reduce.14.cloned.1.call-update) | async-done | bytes 2097168 | tf_op jit(solution)/shard_map/psum | solution.py:163
  919.8 10.4 fusion.18
  930.2 5.4 convert_reduce_fusion.1
  935.6 26.7 %all-reduce.9 = (f32[3,256]{1,0:T(4,128)}, f32[1024]{0:T(1024)S(1)}, f32[1024]{0:T(1024)}, f32[1024]{0:T(1024)S(1)}, f32[1024]{0:T(1024)S(1)}, /*index=5*/f32[1024]{0:T(1024)S(1)}, f32[1024]{0:T(1024)S(1)}) all-reduce(f32[3,256]{1,0:T(4,128)S(1)} %reshape.336, ...), channel_id=1, replica_groups=mesh['fsdp'=2,'ctx'=4,'tp'=4] {'fsdp','ctx'}, use_global_device_ids=true, to_apply=%region_16.17 | all-reduce | flops 6912 | bytes 55296 | tf_op jit(solution)/shard_map/psum | solution.py:258
  964.8 4.0 slice.168
  968.8 1.9 slice.152
  970.6 2.4 slice_bitcast_fusion
  974.1 35.6 %reduce-scatter.11.cloned.1.call-done = f32[128,3,256]{2,0,1:T(8,128)} async-done(((f32[1024,3,256]{2,0,1:T(8,128)}), f32[128,3,256]{2,0,1:T(8,128)}) %reduce-scatter.11.cloned.1.call-update) | async-done | bytes 393232 | tf_op jit(solution)/shard_map/reduce_scatter | solution.py:248
  1009.7 55.1 %reduce-scatter.15.cloned.1.call-done = f32[128,1024]{1,0:T(8,128)} async-done(((f32[1024,1024]{1,0:T(8,128)}), f32[128,1024]{1,0:T(8,128)}) %reduce-scatter.15.cloned.1.call-update) | async-done | bytes 524304 | tf_op jit(solution)/shard_map/reduce_scatter | solution.py:250
  1064.8 55.6 %reduce-scatter.17.cloned.1.call-done = f32[1024,128]{1,0:T(8,128)} async-done(((f32[1024,1024]{1,0:T(8,128)}), f32[1024,128]{1,0:T(8,128)}) %reduce-scatter.17.cloned.1.call-update) | async-done | bytes 524304 | tf_op jit(solution)/shard_map/reduce_scatter | solution.py:251
  (205 shorter events, 29.1 us)
Async XLA Ops:
  7.2 5.6 copy-start
  7.2 7.4 copy-start.44
  7.2 22.1 %copy-start.45 = (bf16[128]{0:T(256)(128)(2,1)S(1)}, bf16[128]{0:T(256)(128)(2,1)}, u32[]{:S(2)}) copy-start(bf16[128]{0:T(256)(128)(2,1)} %param.29) | copy-start | bytes 772
  7.2 35.3 %copy-start.42 = (bf16[3,256]{1,0:T(4,128)(2,1)S(1)}, bf16[3,256]{1,0:T(4,128)(2,1)}, u32[]{:S(2)}) copy-start(bf16[3,256]{1,0:T(4,128)(2,1)} %param.21) | copy-start | bytes 4612
  7.2 35.3 %copy-start.46 = (s32[1,3]{1,0:T(1,128)S(1)}, s32[1,3]{1,0:T(1,128)}, u32[]{:S(2)}) copy-start(s32[1,3]{1,0:T(1,128)} %param.19) | copy-start | bytes 40
  7.2 36.9 %copy-start.29 = (bf16[256,128]{1,0:T(8,128)(2,1)S(1)}, bf16[256,128]{1,0:T(8,128)(2,1)}, u32[]{:S(2)}) copy-start(bf16[256,128]{1,0:T(8,128)(2,1)} %param.22) | copy-start | bytes 196612
  7.2 61.5 %copy-start.47 = (bf16[128]{0:T(256)(128)(2,1)S(1)}, bf16[128]{0:T(256)(128)(2,1)}, u32[]{:S(2)}) copy-start(bf16[128]{0:T(256)(128)(2,1)} %param.30) | copy-start | bytes 772
  7.3 74.6 %copy-start.48 = (bf16[128]{0:T(256)(128)(2,1)S(1)}, bf16[128]{0:T(256)(128)(2,1)}, u32[]{:S(2)}) copy-start(bf16[128]{0:T(256)(128)(2,1)} %param.31) | copy-start | bytes 772
  7.3 89.1 %copy-start.43 = (bf16[1024]{0:T(1024)(128)(2,1)S(1)}, bf16[1024]{0:T(1024)(128)(2,1)}, u32[]{:S(2)}) copy-start(bf16[1024]{0:T(1024)(128)(2,1)} %param.25) | copy-start | bytes 6148
  7.3 89.7 %copy-start.5 = (bf16[1,3,256,1024]{3,2,1,0:T(8,128)(2,1)S(1)}, bf16[1,3,256,1024]{3,2,1,0:T(8,128)(2,1)}, u32[]{:S(2)}) copy-start(bf16[1,3,256,1024]{3,2,1,0:T(8,128)(2,1)} %param.33) | copy-start | bytes 4718596
  7.3 95.3 %all-gather.10.cloned.1.call-start = ((), (), s32[]{:S(2)}) async-start(), calls=%async_computation.6 | async-start | bytes 1769472 | tf_op jit(solution)/shard_map/all_gather | solution.py:78
  9.2 234.9 %all-gather.12.cloned.1.call-start = ((), (), s32[]{:S(2)}) async-start(), calls=%async_computation.7 | async-start | bytes 2359296 | tf_op jit(solution)/shard_map/all_gather | solution.py:80
  10.0 249.8 %all-gather.14.cloned.1.call-start = ((), (), s32[]{:S(2)}) async-start(), calls=%async_computation.8 | async-start | bytes 2359296 | tf_op jit(solution)/shard_map/all_gather | solution.py:81
  10.7 264.0 %reduce-scatter.7.cloned.1.call-start = ((), (), s32[]{:S(2)}) async-start(), calls=%async_computation.10 | async-start | bytes 1310720 | tf_op jit(solution)/shard_map/reduce_scatter | solution.py:206
  12.8 89.8 %copy-start.27 = (f32[1024]{0:T(1024)}, f32[1024]{0:T(1024)S(1)}, u32[]{:S(2)}) copy-start(f32[1024]{0:T(1024)S(1)} %broadcast_multiply_fusion) | copy-start | bytes 12292
  14.5 82.4 %copy-start.33 = (f32[1024]{0:T(1024)}, f32[1024]{0:T(1024)S(1)}, u32[]{:S(2)}) copy-start(f32[1024]{0:T(1024)S(1)} %fusion.19) | copy-start | bytes 12292
  14.6 88.0 %copy-start.35 = (f32[1024]{0:T(1024)}, f32[1024]{0:T(1024)S(1)}, u32[]{:S(2)}) copy-start(f32[1024]{0:T(1024)S(1)} %fusion.55) | copy-start | bytes 12292
  29.3 73.3 %copy-start.30 = (f32[8,1,128]{2,1,0:T(1,128)}, f32[8,1,128]{2,1,0:T(1,128)S(1)}, u32[]{:S(2)}) copy-start(f32[8,1,128]{2,1,0:T(1,128)S(1)} %convert_element_type.144) | copy-start | bytes 12292
  42.5 60.1 %copy-start.39 = (f32[8,1,128]{2,1,0:T(1,128)}, f32[8,1,128]{2,1,0:T(1,128)S(1)}, u32[]{:S(2)}) copy-start(f32[8,1,128]{2,1,0:T(1,128)S(1)} %convert_element_type.145) | copy-start | bytes 12292
  68.7 30.8 %copy-start.15 = (bf16[256,1024]{1,0:T(8,128)(2,1)}, bf16[256,1024]{1,0:T(8,128)(2,1)S(1)}, u32[]{:S(2)}) copy-start(bf16[256,1024]{1,0:T(8,128)(2,1)S(1)} %all_gather.45) | copy-start | bytes 1572868
  106.5 13.9 %copy-start.9 = (bf16[1024,4,48]{0,2,1:T(8,128)(2,1)}, bf16[1024,4,48]{0,2,1:T(8,128)(2,1)S(1)}, u32[]{:S(2)}) copy-start(bf16[1024,4,48]{0,2,1:T(8,128)(2,1)S(1)} %slice.216) | copy-start | bytes 1179652
  107.0 52.9 %copy-start.19 = (bf16[768,4,64]{0,2,1:T(8,128)(2,1)}, bf16[768,4,64]{0,2,1:T(8,128)(2,1)S(1)}, u32[]{:S(2)}) copy-start(bf16[768,4,64]{0,2,1:T(8,128)(2,1)S(1)} %slice_bitcast_fusion.4) | copy-start | bytes 1179652
  120.5 12.9 %copy-start.13 = (bf16[1024,256]{0,1:T(8,128)(2,1)}, bf16[1024,256]{0,1:T(8,128)(2,1)S(1)}, u32[]{:S(2)}) copy-start(bf16[1024,256]{0,1:T(8,128)(2,1)S(1)} %all_gather.44) | copy-start | bytes 1572868
  133.3 26.5 %copy-start.24 = (bf16[1024,256]{0,1:T(8,128)(2,1)S(1)}, bf16[1024,256]{0,1:T(8,128)(2,1)}, u32[]{:S(2)}) copy-start(bf16[1024,256]{0,1:T(8,128)(2,1)} %convolution_convert_fusion.2) | copy-start | bytes 1572868
  159.8 22.0 %copy-start.11 = (bf16[1024,256]{0,1:T(8,128)(2,1)}, bf16[1024,256]{0,1:T(8,128)(2,1)S(1)}, u32[]{:S(2)}) copy-start(bf16[1024,256]{0,1:T(8,128)(2,1)S(1)} %all_gather.43) | copy-start | bytes 1572868
  216.4 63.5 %reduce-scatter.9.cloned.1.call-start = ((), (), s32[]{:S(2)}) async-start(), calls=%async_computation.11 | async-start | bytes 1310720 | tf_op jit(solution)/shard_map/reduce_scatter | solution.py:212
  216.5 15.9 %copy-start.10 = (bf16[1024,4,48]{0,2,1:T(8,128)(2,1)S(1)}, bf16[1024,4,48]{0,2,1:T(8,128)(2,1)}, u32[]{:S(2)}) copy-start(bf16[1024,4,48]{0,2,1:T(8,128)(2,1)} %copy-done.9) | copy-start | bytes 1179652
  216.5 15.9 %copy-start.14 = (bf16[1024,256]{0,1:T(8,128)(2,1)S(1)}, bf16[1024,256]{0,1:T(8,128)(2,1)}, u32[]{:S(2)}) copy-start(bf16[1024,256]{0,1:T(8,128)(2,1)} %copy-done.13) | copy-start | bytes 1572868
  243.9 576.1 %all-reduce.16.cloned.1.call-start = ((), (), s32[]{:S(2)}) async-start(), calls=%async_computation.16 | async-start | bytes 16777216 | tf_op jit(solution)/shard_map/psum | solution.py:242
  244.2 15.7 %copy-start.38 = (f32[1024]{0:T(1024)S(1)}, f32[1024]{0:T(1024)}, u32[]{:S(2)}) copy-start(f32[1024]{0:T(1024)} %convert_element_type.129) | copy-start | bytes 12292
  259.9 10.6 copy-start.51
  287.6 632.2 %all-reduce.14.cloned.1.call-start = ((), (), s32[]{:S(2)}) async-start(), calls=%async_computation.9 | async-start | bytes 4194304 | tf_op jit(solution)/shard_map/psum | solution.py:163
  294.0 680.1 %reduce-scatter.13.cloned.1.call-start = ((), (), s32[]{:S(2)}) async-start(), calls=%async_computation.13 | async-start | bytes 1179648 | tf_op jit(solution)/shard_map/reduce_scatter | solution.py:249
  311.8 697.9 %reduce-scatter.11.cloned.1.call-start = ((), (), s32[]{:S(2)}) async-start(), calls=%async_computation.12 | async-start | bytes 3538944 | tf_op jit(solution)/shard_map/reduce_scatter | solution.py:248
  317.2 747.6 %reduce-scatter.15.cloned.1.call-start = ((), (), s32[]{:S(2)}) async-start(), calls=%async_computation.14 | async-start | bytes 4718592 | tf_op jit(solution)/shard_map/reduce_scatter | solution.py:250
  323.5 797.0 %reduce-scatter.17.cloned.1.call-start = ((), (), s32[]{:S(2)}) async-start(), calls=%async_computation.15 | async-start | bytes 4718592 | tf_op jit(solution)/shard_map/reduce_scatter | solution.py:251
  325.4 197.9 %copy-start.6 = (bf16[1,3,256,1024]{3,2,1,0:T(8,128)(2,1)S(1)}, bf16[1,3,256,1024]{3,2,1,0:T(8,128)(2,1)}, u32[]{:S(2)}) copy-start(bf16[1,3,256,1024]{3,2,1,0:T(8,128)(2,1)} %param.33) | copy-start | bytes 4718596
  325.4 197.8 %copy-start.12 = (bf16[1,256,1024]{2,1,0:T(8,128)(2,1)S(1)}, bf16[1,256,1024]{2,1,0:T(8,128)(2,1)}, u32[]{:S(2)}) copy-start(bf16[1,256,1024]{2,1,0:T(8,128)(2,1)} %param.32) | copy-start | bytes 1572868
  325.4 197.8 %copy-start.17 = (bf16[1024,1024]{1,0:T(8,128)(2,1)S(1)}, bf16[1024,1024]{1,0:T(8,128)(2,1)}, u32[]{:S(2)}) copy-start(bf16[1024,1024]{1,0:T(8,128)(2,1)} %get-tuple-element.37) | copy-start | bytes 6291460
  325.4 194.5 %collective-permute-start = (f32[1024,1024]{1,0:T(8,128)S(1)}, f32[1024,1024]{1,0:T(8,128)S(1)}, u32[]{:S(2)}, u32[]{:S(2)}) collective-permute-start(f32[1024,1024]{1,0:T(8,128)S(1)} %fusion.78), channel_id=1, source_target_pairs={{0,1},{1,0},{2,3},{3,2},{4,5},{5,4},{6,7},{7,6},{8,9},{9,8},{10,11... | collective-permute-start | bytes 12582920 | tf_op jit(solution)/shard_map/ppermute | solution.py:160
  522.8 397.0 %collective-permute-start.1 = (f32[1024,1024]{1,0:T(8,128)}, f32[1024,1024]{1,0:T(8,128)}, u32[]{:S(2)}, u32[]{:S(2)}) collective-permute-start(f32[1024,1024]{1,0:T(8,128)} %add.177), channel_id=1, source_target_pairs={{0,2},{1,3},{2,0},{3,1},{4,6},{5,7},{6,4},{7,5},{8,10},{9,11},{10,... | collective-permute-start | bytes 12582920 | tf_op jit(solution)/shard_map/ppermute | solution.py:160
  527.7 14.2 %copy-start.50 = (bf16[128]{0:T(256)(128)(2,1)S(1)}, bf16[128]{0:T(256)(128)(2,1)}, u32[]{:S(2)}) copy-start(bf16[128]{0:T(256)(128)(2,1)} %param.27) | copy-start | bytes 772
  527.7 27.4 %copy-start.53 = (u32[32]{0:T(128)S(1)}, u32[32]{0:T(128)}, u32[]{:S(2)}) copy-start(u32[32]{0:T(128)} %constant.122) | copy-start | bytes 388
  919.8 10.4 copy-start.1
  919.8 10.4 copy-start.2
  919.8 10.4 copy-start.7
  962.4 6.4 copy-start.3
  962.4 158.0 %copy-start.54 = (f32[128]{0:T(128)}, f32[128]{0:T(128)S(1)}, u32[]{:S(2)}) copy-start(f32[128]{0:T(128)S(1)} %dynamic-slice.1) | copy-start | bytes 1540
  (21 other events, 66.1 us)
Sparse Core Ops, SparseCore 0:
  10.6 28.5 all-gather.9
  41.1 32.1 all-gather.11
  75.2 28.1 all-gather.13
  216.5 27.5 reduce-scatter.6
  247.7 27.7 reduce-scatter.8
  287.8 532.1 all-reduce.15
  822.9 96.8 all-reduce.13
  923.9 35.2 reduce-scatter.12
  963.5 46.1 reduce-scatter.10
  1013.5 51.3 reduce-scatter.14
  1069.1 51.2 reduce-scatter.16
